TPU v7x, 32 devices: a whole 2x2x4 slice. The times are simulated.
32 devices in a mesh: grp: 2 (over x), dev: 16 (over z, y, core).
Axes of the slice: x: 2, y: 2, z: 4, core: 2. Of those that a mesh axis runs over, the one named last changes fastest.
Arguments:
- coords: float32 [16384, 64], P(('grp', 'dev')), may hold values from -6 to 6
- right_side: float32 [16384, 256], P(('grp', 'dev')), may hold values from -6 to 6
- leaf_perm: int32 [32, 512], P(('grp', 'dev')), may hold values from 0 to 511, each once within a row
- near_list: int32 [32, 4], P(('grp', 'dev')), may hold values from -1 to 31, as said below
- far_leaves: int32 [32, 4], P(('grp', 'dev')), may hold values from 0 to 31, as said below
- couplings: bfloat16 [32, 4, 128, 128], P(('grp', 'dev')), may hold values from -0.5 to 0.5
- transfer: bfloat16 [32, 128, 128], P(('grp', 'dev')), may hold values from -0.5 to 0.5
- leaf_basis: bfloat16 [16384, 128], P(('grp', 'dev')), may hold values from -0.25 to 0.25
- cluster_of: int32 [32], P(('grp', 'dev')), may hold values from 0 to 7, as said below
- far_clusters: int32 [8, 4], P('grp'), may hold values from 0 to 7, as said below
- cluster_couplings: bfloat16 [8, 4, 128, 128], P('grp'), may hold values from -0.25 to 0.25
- ridge_weight: float32 [], replicated, may hold values from 0.5 to 2
Outputs:
- solution: float32 [16384, 256], P(('grp', 'dev'))
- residual: float32 [16384, 256], P(('grp', 'dev'))
Inputs may be any that keep to these rules, and one draw needn't show every extreme that they name: `near_list`: each row lists leaves of the row's group whose position within the group differs from the row's leaf by 1 to 2, each at most once, in any slot order; -1 marks an empty slot. The number of listed leaves varies from leaf to leaf. `far_leaves`: each row names 4 different leaves of the row's group whose position within the group differs from the row's leaf by more than 2 and at most 8. `cluster_of`: leaves of group g belong to clusters g * 4 to g * 4 + 3, and every cluster holds exactly 4 leaves. `far_clusters`: each row names 4 different clusters, none of them in the row's own group.
All inputs are finite; a program needn't handle non-finite values.
Results may differ from a plain program's by a relative error of at most 0.0033.
Values may be sent and summed in bfloat16 or wider, within the bound.
A program may use at most 64 MiB of HBM per device.

v0:
```python
import jax
import jax.numpy as jnp
from jax import lax
from jax.sharding import PartitionSpec as P

REACH = 2
FARREACH = 8
ITERS = 2
kernel_scale = 1.0 / 32.0
spectrum_gap = 0.5
spectrum_top = 8.0


def from_behind(shard, axis, by):
    devices = lax.axis_size(axis)
    pairs = [(i, i + by) for i in range(devices) if 0 <= i + by < devices]
    return lax.ppermute(shard, axis, pairs)


def kernel_block(left_points, right_points):
    inner_products = jnp.dot(
        left_points,
        right_points.T,
        precision=lax.Precision.HIGHEST,
        preferred_element_type=jnp.float32,
    )
    distance = (
        jnp.sum(left_points * left_points, axis=1)[:, None]
        + jnp.sum(right_points * right_points, axis=1)[None, :]
        - 2.0 * inner_products
    )
    return jnp.exp(-kernel_scale * distance).astype(jnp.bfloat16)


def body(
    coords,
    right_side,
    leaf_perm,
    near_list,
    far_leaves,
    couplings,
    transfer,
    leaf_basis,
    cluster_of,
    far_clusters,
    cluster_couplings,
    ridge_weight,
):
    dev_count = lax.axis_size("dev")
    group_index = lax.axis_index("grp")
    leaf_id = group_index * dev_count + lax.axis_index("dev")
    clusters_here = far_clusters.shape[0]
    local_cluster = cluster_of[0] - group_index * clusters_here
    ordering = leaf_perm[0]
    near_offsets = [offset for offset in range(-REACH, REACH + 1) if offset != 0]
    far_offsets = [offset for offset in range(-FARREACH, FARREACH + 1) if abs(offset) > REACH]
    neighbours = [from_behind(coords, "dev", -offset) for offset in near_offsets]
    near_flags = [
        jnp.any((near_list[0] == leaf_id + offset) & (near_list[0] >= 0)).astype(jnp.float32)
        for offset in near_offsets
    ]
    far_hits = jnp.stack(
        [far_leaves[0] == leaf_id + offset for offset in far_offsets], axis=1
    ).astype(jnp.bfloat16)
    own_block = kernel_block(coords, coords)
    near_blocks = [kernel_block(coords, neighbour_points) for neighbour_points in neighbours]
    cluster_slots = (jnp.arange(clusters_here) == local_cluster).astype(jnp.float32)

    def operate(direction):
        values = direction.astype(jnp.bfloat16)
        near_sum = jnp.dot(own_block, values, preferred_element_type=jnp.float32)
        for position in range(len(near_offsets)):
            remote = from_behind(values, "dev", -near_offsets[position])
            block_here = near_blocks[position]
            near_term = near_flags[position] * jnp.dot(
                block_here, remote, preferred_element_type=jnp.float32
            )
            near_sum = near_sum + near_term
        skeleton = lax.dot_general(
            leaf_basis,
            values[ordering],
            (((0,), (0,)), ((), ())),
            preferred_element_type=jnp.float32,
        ).astype(jnp.bfloat16)
        remote_skeletons = jnp.stack(
            [from_behind(skeleton, "dev", -offset) for offset in far_offsets]
        )
        chosen = jnp.einsum(
            "kj,jbo->kbo", far_hits, remote_skeletons, preferred_element_type=jnp.float32
        ).astype(jnp.bfloat16)
        level_one = jnp.einsum(
            "kab,kbo->ao", couplings[0], chosen, preferred_element_type=jnp.float32
        )
        uplift = lax.dot_general(
            transfer[0], skeleton, (((0,), (0,)), ((), ())), preferred_element_type=jnp.float32
        )
        contrib = cluster_slots[:, None, None] * uplift[None]
        column_sums = lax.psum_scatter(contrib, "dev", scatter_dimension=2, tiled=True).astype(
            jnp.bfloat16
        )
        every_column = lax.all_gather(column_sums, "grp", axis=0, tiled=True)
        picked = every_column[far_clusters]
        partial_coupled = jnp.einsum(
            "ckab,ckbo->cao", cluster_couplings, picked, preferred_element_type=jnp.float32
        ).astype(jnp.bfloat16)
        whole_columns = lax.all_gather(partial_coupled, "dev", axis=2, tiled=True)
        coupled = whole_columns[local_cluster]
        downward = jnp.dot(transfer[0], coupled, preferred_element_type=jnp.float32)
        tree_rows = jnp.dot(
            leaf_basis,
            (level_one + downward).astype(jnp.bfloat16),
            preferred_element_type=jnp.float32,
        )
        far_part = jnp.zeros_like(tree_rows).at[ordering].set(tree_rows)
        return ridge_weight * direction + (near_sum + far_part)

    bottom_edge = ridge_weight + spectrum_gap
    top_edge = ridge_weight + spectrum_top
    centre = (top_edge + bottom_edge) / 2.0
    spread = (top_edge - bottom_edge) / 2.0
    sigma_ratio = centre / spread
    contraction = 1.0 / sigma_ratio
    direction = right_side / centre
    solution = direction
    residual = right_side
    for rounds in range(ITERS):
        residual = residual - operate(direction)
        rho_next = 1.0 / (2.0 * sigma_ratio - contraction)
        direction = rho_next * contraction * direction + 2.0 * rho_next / spread * residual
        solution = solution + direction
        contraction = rho_next
    return (solution, residual)


def solution(mesh):
    placed = (
        P(("grp", "dev"), None),
        P(("grp", "dev"), None),
        P(("grp", "dev"), None),
        P(("grp", "dev"), None),
        P(("grp", "dev"), None),
        P(("grp", "dev"), None, None, None),
        P(("grp", "dev"), None, None),
        P(("grp", "dev"), None),
        P(("grp", "dev")),
        P("grp", None),
        P("grp", None, None, None),
        P(),
    )
    return jax.shard_map(
        body,
        mesh=mesh,
        in_specs=placed,
        out_specs=(P(("grp", "dev"), None), P(("grp", "dev"), None)),
        check_vma=False,
    )
```

profile of v0, /device:TPU:0, one launch (start us, length us, event | category | flops | bytes accessed | tf_op | source)
XLA Modules:
  0.0 243.9 jit_solution(6696561927409434020)
XLA Ops:
  9.7 2.0 gather_fusion
  12.0 6.0 %collective-permute-start.8 = (bf16[128,256]{0,1:T(8,128)(2,1)S(1)}, bf16[128,256]{0,1:T(8,128)(2,1)S(1)}, u32[]{:S(2)}, u32[]{:S(2)}) collective-permute-start(bf16[128,256]{0,1:T(8,128)(2,1)S(1)} %bitcast.186), channel_id=1, source_target_pairs={{0,8},{1,9},{2,10},{3,11},{4,12},{5,13},{6,14},{7,15},{16,24},{17,... | collective-permute-start | bytes 196616 | tf_op jit(solution)/shard_map/ppermute | solution.py:17
  18.0 3.6 %collective-permute-start.9 = (bf16[128,256]{0,1:T(8,128)(2,1)S(1)}, bf16[128,256]{0,1:T(8,128)(2,1)S(1)}, u32[]{:S(2)}, u32[]{:S(2)}) collective-permute-start(bf16[128,256]{0,1:T(8,128)(2,1)S(1)} %bitcast.187), channel_id=1, source_target_pairs={{0,7},{1,8},{2,9},{3,10},{4,11},{5,12},{6,13},{7,14},{8,15},{16,23... | collective-permute-start | bytes 196616 | tf_op jit(solution)/shard_map/ppermute | solution.py:17
  21.6 2.1 collective-permute-start.10
  23.7 1.3 collective-permute-start.11
  25.0 1.6 collective-permute-start.12
  34.3 2.2 fusion.3
  38.8 2.9 %collective-permute-start.13 = (bf16[128,256]{0,1:T(8,128)(2,1)S(1)}, bf16[128,256]{0,1:T(8,128)(2,1)S(1)}, u32[]{:S(2)}, u32[]{:S(2)}) collective-permute-start(bf16[128,256]{0,1:T(8,128)(2,1)S(1)} %bitcast.191), channel_id=1, source_target_pairs={{0,3},{1,4},{2,5},{3,6},{4,7},{5,8},{6,9},{7,10},{8,11},{9,12},{10... | collective-permute-start | bytes 196616 | tf_op jit(solution)/shard_map/ppermute | solution.py:17
  42.4 1.3 collective-permute-start.14
  44.3 1.3 collective-permute-start.15
  46.2 1.3 collective-permute-start.16
  48.1 1.3 collective-permute-start.17
  50.1 1.3 collective-permute-start.18
  52.0 1.3 collective-permute-start.19
  53.9 2.8 %collective-permute-start.1 = (bf16[512,256]{1,0:T(8,128)(2,1)S(1)}, bf16[512,256]{1,0:T(8,128)(2,1)}, u32[]{:S(2)}, u32[]{:S(2)}) collective-permute-start(bf16[512,256]{1,0:T(8,128)(2,1)S(1)} %fusion.53), channel_id=1, source_target_pairs={{0,2},{1,3},{2,4},{3,5},{4,6},{5,7},{6,8},{7,9},{8,10},{9,11},{10,... | collective-permute-start | bytes 786440 | tf_op jit(solution)/shard_map/ppermute | solution.py:17
  57.4 5.4 %collective-permute-start = (f32[512,64]{0,1:T(8,128)}, f32[512,64]{0,1:T(8,128)S(1)}, u32[]{:S(2)}, u32[]{:S(2)}) collective-permute-start(f32[512,64]{0,1:T(8,128)} %param.12), channel_id=1, source_target_pairs={{0,2},{1,3},{2,4},{3,5},{4,6},{5,7},{6,8},{7,9},{8,10},{9,11},{10,... | collective-permute-start | bytes 393224 | tf_op jit(solution)/shard_map/ppermute | solution.py:17
  63.4 2.8 %collective-permute-start.3 = (bf16[512,256]{1,0:T(8,128)(2,1)S(1)}, bf16[512,256]{1,0:T(8,128)(2,1)}, u32[]{:S(2)}, u32[]{:S(2)}) collective-permute-start(bf16[512,256]{1,0:T(8,128)(2,1)S(1)} %fusion.53), channel_id=1, source_target_pairs={{0,1},{1,2},{2,3},{3,4},{4,5},{5,6},{6,7},{7,8},{8,9},{9,10},{10,1... | collective-permute-start | bytes 786440 | tf_op jit(solution)/shard_map/ppermute | solution.py:17
  66.8 4.2 %collective-permute-start.2 = (f32[512,64]{0,1:T(8,128)}, f32[512,64]{0,1:T(8,128)}, u32[]{:S(2)}, u32[]{:S(2)}) collective-permute-start(f32[512,64]{0,1:T(8,128)} %param.12), channel_id=1, source_target_pairs={{0,1},{1,2},{2,3},{3,4},{4,5},{5,6},{6,7},{7,8},{8,9},{9,10},{10,1... | collective-permute-start | bytes 393224 | tf_op jit(solution)/shard_map/ppermute | solution.py:17
  73.5 2.0 copy.32
  76.7 1.3 collective-permute-start.6
  78.1 2.1 exponential_convert_fusion.3
  80.2 1.3 collective-permute-start.5
  82.4 2.1 exponential_convert_fusion.2
  87.1 2.1 exponential_convert_fusion
  89.3 2.9 %exponential_convert_fusion.1 = bf16[512,512]{1,0:T(8,128)(2,1)} fusion(f32[512]{0:T(512)S(1)} %multiply_reduce_fusion.1, f32[512,64]{0,1:T(8,128)} %param.12, f32[512,64]{0,1:T(8,128)S(1)} %collective-permute-done.4, f32[512]{0:T(512)S(1)} %copy-done.15), kind=kOutput, calls=%fused_computation.58 | convolution fusion | flops 202637312 | bytes 790528 | tf_op jit(solution)/shard_map/dot_general | solution.py:21
  94.7 2.0 fusion.16
  97.6 4.4 %all_gather.12 = bf16[8,128,16]{1,2,0:T(8,128)(2,1)S(1)} all-gather(bf16[4,128,16]{1,2,0:T(8,128)(2,1)S(1)} %convert_element_type.99), channel_id=1, replica_groups=mesh['grp'=2,'dev'=16] {'grp'}, dimensions={0}, use_global_device_ids=true | all-gather | bytes 49152 | tf_op jit(solution)/shard_map/all_gather | solution.py:101
  102.8 28.1 %all_gather.13 = bf16[4,128,256]{1,2,0:T(8,128)(2,1)S(1)} all-gather(bf16[4,128,16]{1,2,0:T(8,128)(2,1)S(1)} %fusion.23), channel_id=1, replica_groups=mesh['grp'=2,'dev'=16] {'dev'}, dimensions={2}, use_global_device_ids=true | all-gather | bytes 278528 | tf_op jit(solution)/shard_map/all_gather | solution.py:106
  132.2 2.9 %scatter_custom_fusion = f32[512,256]{1,0:T(8,128)S(1)} fusion(s32[512]{0:T(512)S(1)} %bitcast.211, f32[512,256]{1,0:T(8,128)} %copy.34, f32[]{:T(128)} %constant.33.clone.1), kind=kCustom, calls=%fused_computation.70 | custom fusion | bytes 524800 | tf_op jit(solution)/shard_map/scatter | solution.py:114
  135.2 2.4 %fusion.24 = (bf16[512,256]{1,0:T(8,128)(2,1)S(1)}, f32[512,256]{1,0:T(8,128)}) fusion(f32[]{:T(128)S(6)} %div.37, f32[]{:T(128)S(6)} %mul.171, f32[512,256]{1,0:T(8,128)S(1)} %copy-done.10, f32[]{:T(128)S(6)} %div.30, f32[512,256]{1,0:T(8,128)S(1)} %scatter_custom_fusion, f32[512,256]{1,0:T(8,128)S(1)} %convolution_multiply_fusion.9, ...), kind=kOutput, calls=%fused_computation.63 | convolution fusion | flops 135790592 | bytes 3670036 | tf_op jit(solution)/shard_map/dot_general | solution.py:75
  137.9 2.0 collective-permute-start.20
  139.9 2.9 %collective-permute-start.21 = (bf16[512,256]{1,0:T(8,128)(2,1)S(1)}, bf16[512,256]{1,0:T(8,128)(2,1)}, u32[]{:S(2)}, u32[]{:S(2)}) collective-permute-start(bf16[512,256]{1,0:T(8,128)(2,1)S(1)} %get-tuple-element.18), channel_id=1, source_target_pairs={{0,1},{1,2},{2,3},{3,4},{4,5},{5,6},{6,7},{7,8},{8,9},{9,10},{10,1... | collective-permute-start | bytes 786440 | tf_op jit(solution)/shard_map/ppermute | solution.py:17
  142.9 1.9 gather_fusion.2
  145.1 1.3 collective-permute-start.24
  146.4 1.3 collective-permute-start.25
  147.7 2.3 collective-permute-start.26
  151.1 1.8 collective-permute-start.27
  153.5 2.3 collective-permute-start.28
  156.5 3.0 %collective-permute-start.29 = (bf16[128,256]{0,1:T(8,128)(2,1)S(1)}, bf16[128,256]{0,1:T(8,128)(2,1)S(1)}, u32[]{:S(2)}, u32[]{:S(2)}) collective-permute-start(bf16[128,256]{0,1:T(8,128)(2,1)S(1)} %bitcast.203), channel_id=1, source_target_pairs={{0,3},{1,4},{2,5},{3,6},{4,7},{5,8},{6,9},{7,10},{8,11},{9,12},{10... | collective-permute-start | bytes 196616 | tf_op jit(solution)/shard_map/ppermute | solution.py:17
  173.5 2.0 collective-permute-done.33
  179.3 5.8 %collective-permute-done.35 = bf16[128,256]{0,1:T(8,128)(2,1)S(1)} collective-permute-done((bf16[128,256]{0,1:T(8,128)(2,1)S(1)}, bf16[128,256]{0,1:T(8,128)(2,1)S(1)}, u32[]{:S(2)}, u32[]{:S(2)}) %collective-permute-start.35) | collective-permute-done | bytes 65568 | tf_op jit(solution)/shard_map/ppermute | solution.py:17
  185.7 2.0 copy.35
  190.9 1.3 convolution_multiply_fusion.5
  193.5 11.7 %reduce-scatter.5.cloned.1.call-done = f32[4,128,16]{1,2,0:T(8,128)} async-done(((f32[4,128,256]{1,2,0:T(8,128)}), f32[4,128,16]{1,2,0:T(8,128)}) %reduce-scatter.5.cloned.1.call-update) | async-done | bytes 32784 | tf_op jit(solution)/shard_map/reduce_scatter | solution.py:98
  206.0 4.4 %all_gather.14 = bf16[8,128,16]{1,2,0:T(8,128)(2,1)S(1)} all-gather(bf16[4,128,16]{1,2,0:T(8,128)(2,1)S(1)} %convert_element_type.107), channel_id=1, replica_groups=mesh['grp'=2,'dev'=16] {'grp'}, dimensions={0}, use_global_device_ids=true | all-gather | bytes 49152 | tf_op jit(solution)/shard_map/all_gather | solution.py:101
  211.2 20.3 %all_gather.15 = bf16[4,128,256]{1,2,0:T(8,128)(2,1)S(1)} all-gather(bf16[4,128,16]{1,2,0:T(8,128)(2,1)S(1)} %fusion.22), channel_id=1, replica_groups=mesh['grp'=2,'dev'=16] {'dev'}, dimensions={2}, use_global_device_ids=true | all-gather | bytes 278528 | tf_op jit(solution)/shard_map/all_gather | solution.py:106
  232.0 2.4 scatter_custom_fusion.1
  234.4 2.7 %add_add_fusion = (f32[512,256]{1,0:T(8,128)}, f32[512,256]{1,0:T(8,128)}) fusion(f32[512,256]{1,0:T(8,128)} %get-tuple-element.19, f32[]{:T(128)S(6)} %div.39, f32[]{:T(128)S(6)} %mul.207, f32[]{:T(128)S(6)} %div.37, f32[]{:T(128)S(6)} %mul.171, f32[512,256]{1,0:T(8,128)S(1)} %copy-done.11, f32[]{:T(128)S(6)} %div.30, ...), kind=kOutput, calls=%fused_computation.61 | convolution fusion | flops 136314880 | bytes 4456476 | tf_op jit(solution)/shard_map/dot_general | solution.py:75
  (170 shorter events, 55.4 us)
Async XLA Ops:
  7.2 95.4 %copy-start = (bf16[4,4,128,128]{3,2,1,0:T(8,128)(2,1)S(1)}, bf16[4,4,128,128]{3,2,1,0:T(8,128)(2,1)}, u32[]{:S(2)}) copy-start(bf16[4,4,128,128]{3,2,1,0:T(8,128)(2,1)} %param.22) | copy-start | bytes 1572868
  7.2 89.6 %reduce-scatter.3.cloned.1.call-start = ((), (), s32[]{:S(2)}) async-start(), calls=%async_computation.2 | async-start | bytes 557056 | tf_op jit(solution)/shard_map/reduce_scatter | solution.py:98
  11.7 15.0 %copy-start.6 = (bf16[1,128,128]{2,1,0:T(8,128)(2,1)S(1)}, bf16[1,128,128]{2,1,0:T(8,128)(2,1)}, u32[]{:S(2)}) copy-start(bf16[1,128,128]{2,1,0:T(8,128)(2,1)} %param.18) | copy-start | bytes 98308
  12.0 26.9 %collective-permute-start.8 = (bf16[128,256]{0,1:T(8,128)(2,1)S(1)}, bf16[128,256]{0,1:T(8,128)(2,1)S(1)}, u32[]{:S(2)}, u32[]{:S(2)}) collective-permute-start(bf16[128,256]{0,1:T(8,128)(2,1)S(1)} %bitcast.186), channel_id=1, source_target_pairs={{0,8},{1,9},{2,10},{3,11},{4,12},{5,13},{6,14},{7,15},{16,24},{17,... | collective-permute-start | bytes 196616 | tf_op jit(solution)/shard_map/ppermute | solution.py:17
  18.0 24.4 %collective-permute-start.9 = (bf16[128,256]{0,1:T(8,128)(2,1)S(1)}, bf16[128,256]{0,1:T(8,128)(2,1)S(1)}, u32[]{:S(2)}, u32[]{:S(2)}) collective-permute-start(bf16[128,256]{0,1:T(8,128)(2,1)S(1)} %bitcast.187), channel_id=1, source_target_pairs={{0,7},{1,8},{2,9},{3,10},{4,11},{5,12},{6,13},{7,14},{8,15},{16,23... | collective-permute-start | bytes 196616 | tf_op jit(solution)/shard_map/ppermute | solution.py:17
  21.6 22.7 %collective-permute-start.10 = (bf16[128,256]{0,1:T(8,128)(2,1)S(1)}, bf16[128,256]{0,1:T(8,128)(2,1)S(1)}, u32[]{:S(2)}, u32[]{:S(2)}) collective-permute-start(bf16[128,256]{0,1:T(8,128)(2,1)S(1)} %bitcast.188), channel_id=1, source_target_pairs={{0,6},{1,7},{2,8},{3,9},{4,10},{5,11},{6,12},{7,13},{8,14},{9,15},... | collective-permute-start | bytes 196616 | tf_op jit(solution)/shard_map/ppermute | solution.py:17
  23.7 22.5 %collective-permute-start.11 = (bf16[128,256]{0,1:T(8,128)(2,1)S(1)}, bf16[128,256]{0,1:T(8,128)(2,1)S(1)}, u32[]{:S(2)}, u32[]{:S(2)}) collective-permute-start(bf16[128,256]{0,1:T(8,128)(2,1)S(1)} %bitcast.189), channel_id=1, source_target_pairs={{0,5},{1,6},{2,7},{3,8},{4,9},{5,10},{6,11},{7,12},{8,13},{9,14},{... | collective-permute-start | bytes 196616 | tf_op jit(solution)/shard_map/ppermute | solution.py:17
  25.0 23.1 %collective-permute-start.12 = (bf16[128,256]{0,1:T(8,128)(2,1)S(1)}, bf16[128,256]{0,1:T(8,128)(2,1)S(1)}, u32[]{:S(2)}, u32[]{:S(2)}) collective-permute-start(bf16[128,256]{0,1:T(8,128)(2,1)S(1)} %bitcast.190), channel_id=1, source_target_pairs={{0,4},{1,5},{2,6},{3,7},{4,8},{5,9},{6,10},{7,11},{8,12},{9,13},{1... | collective-permute-start | bytes 196616 | tf_op jit(solution)/shard_map/ppermute | solution.py:17
  28.4 176.8 %reduce-scatter.5.cloned.1.call-start = ((), (), s32[]{:S(2)}) async-start(), calls=%async_computation.3 | async-start | bytes 557056 | tf_op jit(solution)/shard_map/reduce_scatter | solution.py:98
  38.8 11.2 %collective-permute-start.13 = (bf16[128,256]{0,1:T(8,128)(2,1)S(1)}, bf16[128,256]{0,1:T(8,128)(2,1)S(1)}, u32[]{:S(2)}, u32[]{:S(2)}) collective-permute-start(bf16[128,256]{0,1:T(8,128)(2,1)S(1)} %bitcast.191), channel_id=1, source_target_pairs={{0,3},{1,4},{2,5},{3,6},{4,7},{5,8},{6,9},{7,10},{8,11},{9,12},{10... | collective-permute-start | bytes 196616 | tf_op jit(solution)/shard_map/ppermute | solution.py:17
  42.4 9.6 %collective-permute-start.14 = (bf16[128,256]{0,1:T(8,128)(2,1)S(1)}, bf16[128,256]{0,1:T(8,128)(2,1)S(1)}, u32[]{:S(2)}, u32[]{:S(2)}) collective-permute-start(bf16[128,256]{0,1:T(8,128)(2,1)S(1)} %bitcast.192), channel_id=1, source_target_pairs={{3,0},{4,1},{5,2},{6,3},{7,4},{8,5},{9,6},{10,7},{11,8},{12,9},{13... | collective-permute-start | bytes 196616 | tf_op jit(solution)/shard_map/ppermute | solution.py:17
  44.3 9.6 %collective-permute-start.15 = (bf16[128,256]{0,1:T(8,128)(2,1)S(1)}, bf16[128,256]{0,1:T(8,128)(2,1)S(1)}, u32[]{:S(2)}, u32[]{:S(2)}) collective-permute-start(bf16[128,256]{0,1:T(8,128)(2,1)S(1)} %bitcast.193), channel_id=1, source_target_pairs={{4,0},{5,1},{6,2},{7,3},{8,4},{9,5},{10,6},{11,7},{12,8},{13,9},{1... | collective-permute-start | bytes 196616 | tf_op jit(solution)/shard_map/ppermute | solution.py:17
  46.2 11.1 %collective-permute-start.16 = (bf16[128,256]{0,1:T(8,128)(2,1)S(1)}, bf16[128,256]{0,1:T(8,128)(2,1)S(1)}, u32[]{:S(2)}, u32[]{:S(2)}) collective-permute-start(bf16[128,256]{0,1:T(8,128)(2,1)S(1)} %bitcast.194), channel_id=1, source_target_pairs={{5,0},{6,1},{7,2},{8,3},{9,4},{10,5},{11,6},{12,7},{13,8},{14,9},{... | collective-permute-start | bytes 196616 | tf_op jit(solution)/shard_map/ppermute | solution.py:17
  48.1 15.2 %collective-permute-start.17 = (bf16[128,256]{0,1:T(8,128)(2,1)S(1)}, bf16[128,256]{0,1:T(8,128)(2,1)S(1)}, u32[]{:S(2)}, u32[]{:S(2)}) collective-permute-start(bf16[128,256]{0,1:T(8,128)(2,1)S(1)} %bitcast.195), channel_id=1, source_target_pairs={{6,0},{7,1},{8,2},{9,3},{10,4},{11,5},{12,6},{13,7},{14,8},{15,9},... | collective-permute-start | bytes 196616 | tf_op jit(solution)/shard_map/ppermute | solution.py:17
  50.1 16.8 %collective-permute-start.18 = (bf16[128,256]{0,1:T(8,128)(2,1)S(1)}, bf16[128,256]{0,1:T(8,128)(2,1)S(1)}, u32[]{:S(2)}, u32[]{:S(2)}) collective-permute-start(bf16[128,256]{0,1:T(8,128)(2,1)S(1)} %bitcast.196), channel_id=1, source_target_pairs={{7,0},{8,1},{9,2},{10,3},{11,4},{12,5},{13,6},{14,7},{15,8},{23,16... | collective-permute-start | bytes 196616 | tf_op jit(solution)/shard_map/ppermute | solution.py:17
  52.0 19.6 %collective-permute-start.19 = (bf16[128,256]{0,1:T(8,128)(2,1)S(1)}, bf16[128,256]{0,1:T(8,128)(2,1)S(1)}, u32[]{:S(2)}, u32[]{:S(2)}) collective-permute-start(bf16[128,256]{0,1:T(8,128)(2,1)S(1)} %bitcast.197), channel_id=1, source_target_pairs={{8,0},{9,1},{10,2},{11,3},{12,4},{13,5},{14,6},{15,7},{24,16},{25,... | collective-permute-start | bytes 196616 | tf_op jit(solution)/shard_map/ppermute | solution.py:17
  53.9 38.3 %collective-permute-start.1 = (bf16[512,256]{1,0:T(8,128)(2,1)S(1)}, bf16[512,256]{1,0:T(8,128)(2,1)}, u32[]{:S(2)}, u32[]{:S(2)}) collective-permute-start(bf16[512,256]{1,0:T(8,128)(2,1)S(1)} %fusion.53), channel_id=1, source_target_pairs={{0,2},{1,3},{2,4},{3,5},{4,6},{5,7},{6,8},{7,9},{8,10},{9,11},{10,... | collective-permute-start | bytes 786440 | tf_op jit(solution)/shard_map/ppermute | solution.py:17
  57.4 19.4 %collective-permute-start = (f32[512,64]{0,1:T(8,128)}, f32[512,64]{0,1:T(8,128)S(1)}, u32[]{:S(2)}, u32[]{:S(2)}) collective-permute-start(f32[512,64]{0,1:T(8,128)} %param.12), channel_id=1, source_target_pairs={{0,2},{1,3},{2,4},{3,5},{4,6},{5,7},{6,8},{7,9},{8,10},{9,11},{10,... | collective-permute-start | bytes 393224 | tf_op jit(solution)/shard_map/ppermute | solution.py:17
  63.4 31.3 %collective-permute-start.3 = (bf16[512,256]{1,0:T(8,128)(2,1)S(1)}, bf16[512,256]{1,0:T(8,128)(2,1)}, u32[]{:S(2)}, u32[]{:S(2)}) collective-permute-start(bf16[512,256]{1,0:T(8,128)(2,1)S(1)} %fusion.53), channel_id=1, source_target_pairs={{0,1},{1,2},{2,3},{3,4},{4,5},{5,6},{6,7},{7,8},{8,9},{9,10},{10,1... | collective-permute-start | bytes 786440 | tf_op jit(solution)/shard_map/ppermute | solution.py:17
  66.8 13.4 %collective-permute-start.2 = (f32[512,64]{0,1:T(8,128)}, f32[512,64]{0,1:T(8,128)}, u32[]{:S(2)}, u32[]{:S(2)}) collective-permute-start(f32[512,64]{0,1:T(8,128)} %param.12), channel_id=1, source_target_pairs={{0,1},{1,2},{2,3},{3,4},{4,5},{5,6},{6,7},{7,8},{8,9},{9,10},{10,1... | collective-permute-start | bytes 393224 | tf_op jit(solution)/shard_map/ppermute | solution.py:17
  71.6 21.9 %collective-permute-start.7 = (bf16[512,256]{1,0:T(8,128)(2,1)S(1)}, bf16[512,256]{1,0:T(8,128)(2,1)}, u32[]{:S(2)}, u32[]{:S(2)}) collective-permute-start(bf16[512,256]{1,0:T(8,128)(2,1)S(1)} %fusion.53), channel_id=1, source_target_pairs={{2,0},{3,1},{4,2},{5,3},{6,4},{7,5},{8,6},{9,7},{10,8},{11,9},{12,... | collective-permute-start | bytes 786440 | tf_op jit(solution)/shard_map/ppermute | solution.py:17
  76.7 9.1 %collective-permute-start.6 = (f32[512,64]{0,1:T(8,128)}, f32[512,64]{0,1:T(8,128)S(1)}, u32[]{:S(2)}, u32[]{:S(2)}) collective-permute-start(f32[512,64]{0,1:T(8,128)} %param.12), channel_id=1, source_target_pairs={{2,0},{3,1},{4,2},{5,3},{6,4},{7,5},{8,6},{9,7},{10,8},{11,9},{12,... | collective-permute-start | bytes 393224 | tf_op jit(solution)/shard_map/ppermute | solution.py:17
  80.2 12.0 %copy-start.4 = (bf16[512,512]{1,0:T(8,128)(2,1)}, bf16[512,512]{1,0:T(8,128)(2,1)S(1)}, u32[]{:S(2)}) copy-start(bf16[512,512]{1,0:T(8,128)(2,1)S(1)} %exponential_convert_fusion.3) | copy-start | bytes 1572868
  80.2 55.0 %collective-permute-start.5 = (bf16[512,256]{1,0:T(8,128)(2,1)S(1)}, bf16[512,256]{1,0:T(8,128)(2,1)}, u32[]{:S(2)}, u32[]{:S(2)}) collective-permute-start(bf16[512,256]{1,0:T(8,128)(2,1)S(1)} %fusion.53), channel_id=1, source_target_pairs={{1,0},{2,1},{3,2},{4,3},{5,4},{6,5},{7,6},{8,7},{9,8},{10,9},{11,1... | collective-permute-start | bytes 786440 | tf_op jit(solution)/shard_map/ppermute | solution.py:17
  84.6 10.2 %copy-start.2 = (bf16[512,512]{1,0:T(8,128)(2,1)}, bf16[512,512]{1,0:T(8,128)(2,1)S(1)}, u32[]{:S(2)}) copy-start(bf16[512,512]{1,0:T(8,128)(2,1)S(1)} %exponential_convert_fusion.2) | copy-start | bytes 1572868
  85.8 3.4 %collective-permute-start.4 = (f32[512,64]{0,1:T(8,128)}, f32[512,64]{0,1:T(8,128)S(1)}, u32[]{:S(2)}, u32[]{:S(2)}) collective-permute-start(f32[512,64]{0,1:T(8,128)} %param.12), channel_id=1, source_target_pairs={{1,0},{2,1},{3,2},{4,3},{5,4},{6,5},{7,6},{8,7},{9,8},{10,9},{11,1... | collective-permute-start | bytes 393224 | tf_op jit(solution)/shard_map/ppermute | solution.py:17
  102.8 28.1 %copy-start.7 = (bf16[1,128,128]{2,1,0:T(8,128)(2,1)S(1)}, bf16[1,128,128]{2,1,0:T(8,128)(2,1)}, u32[]{:S(2)}) copy-start(bf16[1,128,128]{2,1,0:T(8,128)(2,1)} %param.18) | copy-start | bytes 98308
  132.2 2.9 %copy-start.10 = (f32[512,256]{1,0:T(8,128)S(1)}, f32[512,256]{1,0:T(8,128)}, u32[]{:S(2)}) copy-start(f32[512,256]{1,0:T(8,128)} %param.13) | copy-start | bytes 1572868
  137.9 50.9 %collective-permute-start.20 = (bf16[512,256]{1,0:T(8,128)(2,1)S(1)}, bf16[512,256]{1,0:T(8,128)(2,1)}, u32[]{:S(2)}, u32[]{:S(2)}) collective-permute-start(bf16[512,256]{1,0:T(8,128)(2,1)S(1)} %get-tuple-element.18), channel_id=1, source_target_pairs={{0,2},{1,3},{2,4},{3,5},{4,6},{5,7},{6,8},{7,9},{8,10},{9,11},{10,... | collective-permute-start | bytes 786440 | tf_op jit(solution)/shard_map/ppermute | solution.py:17
  139.9 52.3 %collective-permute-start.21 = (bf16[512,256]{1,0:T(8,128)(2,1)S(1)}, bf16[512,256]{1,0:T(8,128)(2,1)}, u32[]{:S(2)}, u32[]{:S(2)}) collective-permute-start(bf16[512,256]{1,0:T(8,128)(2,1)S(1)} %get-tuple-element.18), channel_id=1, source_target_pairs={{0,1},{1,2},{2,3},{3,4},{4,5},{5,6},{6,7},{7,8},{8,9},{9,10},{10,1... | collective-permute-start | bytes 786440 | tf_op jit(solution)/shard_map/ppermute | solution.py:17
  144.8 5.2 %copy-start.8 = (bf16[1,128,128]{2,1,0:T(8,128)(2,1)S(1)}, bf16[1,128,128]{2,1,0:T(8,128)(2,1)}, u32[]{:S(2)}) copy-start(bf16[1,128,128]{2,1,0:T(8,128)(2,1)} %param.18) | copy-start | bytes 98308
  145.1 5.0 %copy-start.19 = (f32[4]{0:T(128)S(1)}, f32[4]{0:T(128)}, u32[]{:S(2)}) copy-start(f32[4]{0:T(128)} %copy-done.18) | copy-start | bytes 52
  145.1 6.0 %collective-permute-start.24 = (bf16[128,256]{0,1:T(8,128)(2,1)S(1)}, bf16[128,256]{0,1:T(8,128)(2,1)S(1)}, u32[]{:S(2)}, u32[]{:S(2)}) collective-permute-start(bf16[128,256]{0,1:T(8,128)(2,1)S(1)} %bitcast.198), channel_id=1, source_target_pairs={{0,8},{1,9},{2,10},{3,11},{4,12},{5,13},{6,14},{7,15},{16,24},{17,... | collective-permute-start | bytes 196616 | tf_op jit(solution)/shard_map/ppermute | solution.py:17
  146.4 7.1 %collective-permute-start.25 = (bf16[128,256]{0,1:T(8,128)(2,1)S(1)}, bf16[128,256]{0,1:T(8,128)(2,1)S(1)}, u32[]{:S(2)}, u32[]{:S(2)}) collective-permute-start(bf16[128,256]{0,1:T(8,128)(2,1)S(1)} %bitcast.199), channel_id=1, source_target_pairs={{0,7},{1,8},{2,9},{3,10},{4,11},{5,12},{6,13},{7,14},{8,15},{16,23... | collective-permute-start | bytes 196616 | tf_op jit(solution)/shard_map/ppermute | solution.py:17
  147.7 8.8 %collective-permute-start.26 = (bf16[128,256]{0,1:T(8,128)(2,1)S(1)}, bf16[128,256]{0,1:T(8,128)(2,1)S(1)}, u32[]{:S(2)}, u32[]{:S(2)}) collective-permute-start(bf16[128,256]{0,1:T(8,128)(2,1)S(1)} %bitcast.200), channel_id=1, source_target_pairs={{0,6},{1,7},{2,8},{3,9},{4,10},{5,11},{6,12},{7,13},{8,14},{9,15},... | collective-permute-start | bytes 196616 | tf_op jit(solution)/shard_map/ppermute | solution.py:17
  151.1 9.0 %collective-permute-start.27 = (bf16[128,256]{0,1:T(8,128)(2,1)S(1)}, bf16[128,256]{0,1:T(8,128)(2,1)S(1)}, u32[]{:S(2)}, u32[]{:S(2)}) collective-permute-start(bf16[128,256]{0,1:T(8,128)(2,1)S(1)} %bitcast.201), channel_id=1, source_target_pairs={{0,5},{1,6},{2,7},{3,8},{4,9},{5,10},{6,11},{7,12},{8,13},{9,14},{... | collective-permute-start | bytes 196616 | tf_op jit(solution)/shard_map/ppermute | solution.py:17
  153.5 8.5 %collective-permute-start.28 = (bf16[128,256]{0,1:T(8,128)(2,1)S(1)}, bf16[128,256]{0,1:T(8,128)(2,1)S(1)}, u32[]{:S(2)}, u32[]{:S(2)}) collective-permute-start(bf16[128,256]{0,1:T(8,128)(2,1)S(1)} %bitcast.202), channel_id=1, source_target_pairs={{0,4},{1,5},{2,6},{3,7},{4,8},{5,9},{6,10},{7,11},{8,12},{9,13},{1... | collective-permute-start | bytes 196616 | tf_op jit(solution)/shard_map/ppermute | solution.py:17
  156.5 7.5 %collective-permute-start.29 = (bf16[128,256]{0,1:T(8,128)(2,1)S(1)}, bf16[128,256]{0,1:T(8,128)(2,1)S(1)}, u32[]{:S(2)}, u32[]{:S(2)}) collective-permute-start(bf16[128,256]{0,1:T(8,128)(2,1)S(1)} %bitcast.203), channel_id=1, source_target_pairs={{0,3},{1,4},{2,5},{3,6},{4,7},{5,8},{6,9},{7,10},{8,11},{9,12},{10... | collective-permute-start | bytes 196616 | tf_op jit(solution)/shard_map/ppermute | solution.py:17
  160.1 5.8 %collective-permute-start.30 = (bf16[128,256]{0,1:T(8,128)(2,1)S(1)}, bf16[128,256]{0,1:T(8,128)(2,1)S(1)}, u32[]{:S(2)}, u32[]{:S(2)}) collective-permute-start(bf16[128,256]{0,1:T(8,128)(2,1)S(1)} %bitcast.204), channel_id=1, source_target_pairs={{3,0},{4,1},{5,2},{6,3},{7,4},{8,5},{9,6},{10,7},{11,8},{12,9},{13... | collective-permute-start | bytes 196616 | tf_op jit(solution)/shard_map/ppermute | solution.py:17
  162.1 6.8 %collective-permute-start.31 = (bf16[128,256]{0,1:T(8,128)(2,1)S(1)}, bf16[128,256]{0,1:T(8,128)(2,1)S(1)}, u32[]{:S(2)}, u32[]{:S(2)}) collective-permute-start(bf16[128,256]{0,1:T(8,128)(2,1)S(1)} %bitcast.205), channel_id=1, source_target_pairs={{4,0},{5,1},{6,2},{7,3},{8,4},{9,5},{10,6},{11,7},{12,8},{13,9},{1... | collective-permute-start | bytes 196616 | tf_op jit(solution)/shard_map/ppermute | solution.py:17
  164.0 7.6 %collective-permute-start.32 = (bf16[128,256]{0,1:T(8,128)(2,1)S(1)}, bf16[128,256]{0,1:T(8,128)(2,1)S(1)}, u32[]{:S(2)}, u32[]{:S(2)}) collective-permute-start(bf16[128,256]{0,1:T(8,128)(2,1)S(1)} %bitcast.206), channel_id=1, source_target_pairs={{5,0},{6,1},{7,2},{8,3},{9,4},{10,5},{11,6},{12,7},{13,8},{14,9},{... | collective-permute-start | bytes 196616 | tf_op jit(solution)/shard_map/ppermute | solution.py:17
  165.9 9.6 %collective-permute-start.33 = (bf16[128,256]{0,1:T(8,128)(2,1)S(1)}, bf16[128,256]{0,1:T(8,128)(2,1)S(1)}, u32[]{:S(2)}, u32[]{:S(2)}) collective-permute-start(bf16[128,256]{0,1:T(8,128)(2,1)S(1)} %bitcast.207), channel_id=1, source_target_pairs={{6,0},{7,1},{8,2},{9,3},{10,4},{11,5},{12,6},{13,7},{14,8},{15,9},... | collective-permute-start | bytes 196616 | tf_op jit(solution)/shard_map/ppermute | solution.py:17
  168.8 8.5 %collective-permute-start.34 = (bf16[128,256]{0,1:T(8,128)(2,1)S(1)}, bf16[128,256]{0,1:T(8,128)(2,1)S(1)}, u32[]{:S(2)}, u32[]{:S(2)}) collective-permute-start(bf16[128,256]{0,1:T(8,128)(2,1)S(1)} %bitcast.208), channel_id=1, source_target_pairs={{7,0},{8,1},{9,2},{10,3},{11,4},{12,5},{13,6},{14,7},{15,8},{23,16... | collective-permute-start | bytes 196616 | tf_op jit(solution)/shard_map/ppermute | solution.py:17
  171.5 13.5 %collective-permute-start.35 = (bf16[128,256]{0,1:T(8,128)(2,1)S(1)}, bf16[128,256]{0,1:T(8,128)(2,1)S(1)}, u32[]{:S(2)}, u32[]{:S(2)}) collective-permute-start(bf16[128,256]{0,1:T(8,128)(2,1)S(1)} %bitcast.209), channel_id=1, source_target_pairs={{8,0},{9,1},{10,2},{11,3},{12,4},{13,5},{14,6},{15,7},{24,16},{25,... | collective-permute-start | bytes 196616 | tf_op jit(solution)/shard_map/ppermute | solution.py:17
  175.5 15.5 %collective-permute-start.23 = (bf16[512,256]{1,0:T(8,128)(2,1)S(1)}, bf16[512,256]{1,0:T(8,128)(2,1)}, u32[]{:S(2)}, u32[]{:S(2)}) collective-permute-start(bf16[512,256]{1,0:T(8,128)(2,1)S(1)} %get-tuple-element.18), channel_id=1, source_target_pairs={{2,0},{3,1},{4,2},{5,3},{6,4},{7,5},{8,6},{9,7},{10,8},{11,9},{12,... | collective-permute-start | bytes 786440 | tf_op jit(solution)/shard_map/ppermute | solution.py:17
  177.4 57.0 %collective-permute-start.22 = (bf16[512,256]{1,0:T(8,128)(2,1)S(1)}, bf16[512,256]{1,0:T(8,128)(2,1)}, u32[]{:S(2)}, u32[]{:S(2)}) collective-permute-start(bf16[512,256]{1,0:T(8,128)(2,1)S(1)} %get-tuple-element.18), channel_id=1, source_target_pairs={{1,0},{2,1},{3,2},{4,3},{5,4},{6,5},{7,6},{8,7},{9,8},{10,9},{11,1... | collective-permute-start | bytes 786440 | tf_op jit(solution)/shard_map/ppermute | solution.py:17
  211.2 20.3 %copy-start.9 = (bf16[1,128,128]{2,1,0:T(8,128)(2,1)S(1)}, bf16[1,128,128]{2,1,0:T(8,128)(2,1)}, u32[]{:S(2)}) copy-start(bf16[1,128,128]{2,1,0:T(8,128)(2,1)} %param.18) | copy-start | bytes 98308
  232.0 2.4 copy-start.11
  (12 other events, 13.3 us)
Sparse Core Ops, SparseCore 0:
  28.5 57.2 reduce-scatter.2
  151.2 53.9 reduce-scatter.4
where the time goes:
time: 246 us; the launch traced here: 244 us
  starting transfers between devices  72.8 us (30%)
  blocking collectives  57.2 us (23%)
  local copies, waits for them, and re-layouts  36.7 us (15%)
  matrix products  28.5 us (12%)
  waiting for transfers between devices  22.6 us (9%)
  between operations  19 us (8%)
  other arithmetic  7.11 us (3%)
    ppermute x36, starting transfers between devices, from_behind(): return lax.ppermute(shard, axis, pairs)  72.7 us
    all_gather x2, blocking collectives, operate(): whole_columns = lax.all_gather(partial_coupled, 'dev', axis=2, tiled=True)  48.4 us
    unnamed x66, local copies, waits for them, and re-layouts  18.5 us
    dot_general x8, matrix products, operate(): jnp.dot(block_here, remote, preferred_element_type=jnp.float32)  13.5 us
    reduce_scatter x2, waiting for transfers between devices, operate(): lax.psum_scatter(contrib, 'dev', scatter_dimension=2, tiled=True)  11.7 us
    dot_general x5, matrix products, kernel_block(): jnp.dot(left_points, right_points.T, precision=lax.Precision.HIGHEST, pre...  11.4 us
    ppermute x36, waiting for transfers between devices, from_behind(): return lax.ppermute(shard, axis, pairs)  10.9 us
    all_gather x2, blocking collectives, operate(): every_column = lax.all_gather(column_sums, 'grp', axis=0, tiled=True)  8.79 us
  transfers between devices with their start and end apart: 38, of which 6 were waited for; matrix products, arithmetic and copies ran while one was open for 24% of the time, Pallas kernels for 0%

commit v1 on v0

--- a/solution.py
+++ b/solution.py
@@ -103,7 +103,7 @@
         partial_coupled = jnp.einsum(
             "ckab,ckbo->cao", cluster_couplings, picked, preferred_element_type=jnp.float32
         ).astype(jnp.bfloat16)
-        whole_columns = lax.all_gather(partial_coupled, "dev", axis=2, tiled=True)
+        whole_columns = jnp.concatenate(lax.all_gather(partial_coupled, "dev"), axis=2)
         coupled = whole_columns[local_cluster]
         downward = jnp.dot(transfer[0], coupled, preferred_element_type=jnp.float32)
         tree_rows = jnp.dot(

time: 246 us -> 247 us (level)
  no operation moved by 1% of the time
where the time goes in v1:
time: 247 us; the launch traced here: 245 us
  starting transfers between devices  72.8 us (29%)
  blocking collectives  56.9 us (23%)
  local copies, waits for them, and re-layouts  38.2 us (15%)
  matrix products  28.5 us (12%)
  waiting for transfers between devices  22.6 us (9%)
  between operations  19 us (8%)
  other arithmetic  7.11 us (3%)
    ppermute x36, starting transfers between devices, from_behind(): return lax.ppermute(shard, axis, pairs)  72.7 us
    all_gather x2, blocking collectives, operate(): lax.all_gather(partial_coupled, 'dev')  48.1 us
    unnamed x66, local copies, waits for them, and re-layouts  19.9 us
    dot_general x8, matrix products, operate(): jnp.dot(block_here, remote, preferred_element_type=jnp.float32)  13.5 us
    reduce_scatter x2, waiting for transfers between devices, operate(): lax.psum_scatter(contrib, 'dev', scatter_dimension=2, tiled=True)  11.7 us
    dot_general x5, matrix products, kernel_block(): jnp.dot(left_points, right_points.T, precision=lax.Precision.HIGHEST, pre...  11.4 us
    ppermute x36, waiting for transfers between devices, from_behind(): return lax.ppermute(shard, axis, pairs)  10.9 us
    all_gather x2, blocking collectives, operate(): every_column = lax.all_gather(column_sums, 'grp', axis=0, tiled=True)  8.79 us
  transfers between devices with their start and end apart: 38, of which 6 were waited for; matrix products, arithmetic and copies ran while one was open for 24% of the time, Pallas kernels for 0%

profile of v1, /device:TPU:0, one launch (start us, length us, event | category | flops | bytes accessed | tf_op | source)
XLA Modules:
  0.0 245.2 jit_solution(18075444719402892215)
XLA Ops:
  9.7 2.0 gather_fusion
  12.0 6.0 %collective-permute-start.8 = (bf16[128,256]{0,1:T(8,128)(2,1)S(1)}, bf16[128,256]{0,1:T(8,128)(2,1)S(1)}, u32[]{:S(2)}, u32[]{:S(2)}) collective-permute-start(bf16[128,256]{0,1:T(8,128)(2,1)S(1)} %bitcast.198), channel_id=1, source_target_pairs={{0,8},{1,9},{2,10},{3,11},{4,12},{5,13},{6,14},{7,15},{16,24},{17,... | collective-permute-start | bytes 196616 | tf_op jit(solution)/shard_map/ppermute | solution.py:17
  18.0 3.6 %collective-permute-start.9 = (bf16[128,256]{0,1:T(8,128)(2,1)S(1)}, bf16[128,256]{0,1:T(8,128)(2,1)S(1)}, u32[]{:S(2)}, u32[]{:S(2)}) collective-permute-start(bf16[128,256]{0,1:T(8,128)(2,1)S(1)} %bitcast.199), channel_id=1, source_target_pairs={{0,7},{1,8},{2,9},{3,10},{4,11},{5,12},{6,13},{7,14},{8,15},{16,23... | collective-permute-start | bytes 196616 | tf_op jit(solution)/shard_map/ppermute | solution.py:17
  21.6 2.1 collective-permute-start.10
  23.7 1.3 collective-permute-start.11
  25.0 1.6 collective-permute-start.12
  34.3 2.2 fusion.3
  38.8 2.9 %collective-permute-start.13 = (bf16[128,256]{0,1:T(8,128)(2,1)S(1)}, bf16[128,256]{0,1:T(8,128)(2,1)S(1)}, u32[]{:S(2)}, u32[]{:S(2)}) collective-permute-start(bf16[128,256]{0,1:T(8,128)(2,1)S(1)} %bitcast.203), channel_id=1, source_target_pairs={{0,3},{1,4},{2,5},{3,6},{4,7},{5,8},{6,9},{7,10},{8,11},{9,12},{10... | collective-permute-start | bytes 196616 | tf_op jit(solution)/shard_map/ppermute | solution.py:17
  42.4 1.3 collective-permute-start.14
  44.3 1.3 collective-permute-start.15
  46.2 1.3 collective-permute-start.16
  48.1 1.3 collective-permute-start.17
  50.1 1.3 collective-permute-start.18
  52.0 1.3 collective-permute-start.19
  53.9 2.8 %collective-permute-start.1 = (bf16[512,256]{1,0:T(8,128)(2,1)S(1)}, bf16[512,256]{1,0:T(8,128)(2,1)}, u32[]{:S(2)}, u32[]{:S(2)}) collective-permute-start(bf16[512,256]{1,0:T(8,128)(2,1)S(1)} %fusion.53), channel_id=1, source_target_pairs={{0,2},{1,3},{2,4},{3,5},{4,6},{5,7},{6,8},{7,9},{8,10},{9,11},{10,... | collective-permute-start | bytes 786440 | tf_op jit(solution)/shard_map/ppermute | solution.py:17
  57.4 5.4 %collective-permute-start = (f32[512,64]{0,1:T(8,128)}, f32[512,64]{0,1:T(8,128)S(1)}, u32[]{:S(2)}, u32[]{:S(2)}) collective-permute-start(f32[512,64]{0,1:T(8,128)} %param.12), channel_id=1, source_target_pairs={{0,2},{1,3},{2,4},{3,5},{4,6},{5,7},{6,8},{7,9},{8,10},{9,11},{10,... | collective-permute-start | bytes 393224 | tf_op jit(solution)/shard_map/ppermute | solution.py:17
  63.4 2.8 %collective-permute-start.3 = (bf16[512,256]{1,0:T(8,128)(2,1)S(1)}, bf16[512,256]{1,0:T(8,128)(2,1)}, u32[]{:S(2)}, u32[]{:S(2)}) collective-permute-start(bf16[512,256]{1,0:T(8,128)(2,1)S(1)} %fusion.53), channel_id=1, source_target_pairs={{0,1},{1,2},{2,3},{3,4},{4,5},{5,6},{6,7},{7,8},{8,9},{9,10},{10,1... | collective-permute-start | bytes 786440 | tf_op jit(solution)/shard_map/ppermute | solution.py:17
  66.8 4.2 %collective-permute-start.2 = (f32[512,64]{0,1:T(8,128)}, f32[512,64]{0,1:T(8,128)}, u32[]{:S(2)}, u32[]{:S(2)}) collective-permute-start(f32[512,64]{0,1:T(8,128)} %param.12), channel_id=1, source_target_pairs={{0,1},{1,2},{2,3},{3,4},{4,5},{5,6},{6,7},{7,8},{8,9},{9,10},{10,1... | collective-permute-start | bytes 393224 | tf_op jit(solution)/shard_map/ppermute | solution.py:17
  73.5 2.0 copy.52
  76.7 1.3 collective-permute-start.6
  78.1 2.1 exponential_convert_fusion.3
  80.2 1.3 collective-permute-start.5
  82.4 2.1 exponential_convert_fusion.2
  87.1 2.1 exponential_convert_fusion
  89.3 2.9 %exponential_convert_fusion.1 = bf16[512,512]{1,0:T(8,128)(2,1)} fusion(f32[512]{0:T(512)S(1)} %multiply_reduce_fusion.1, f32[512,64]{0,1:T(8,128)} %param.12, f32[512,64]{0,1:T(8,128)S(1)} %collective-permute-done.4, f32[512]{0:T(512)S(1)} %copy-done.15), kind=kOutput, calls=%fused_computation.58 | convolution fusion | flops 202637312 | bytes 790528 | tf_op jit(solution)/shard_map/dot_general | solution.py:21
  94.7 2.0 fusion.16
  97.6 4.4 %all_gather.18 = bf16[8,128,16]{1,2,0:T(8,128)(2,1)S(1)} all-gather(bf16[4,128,16]{1,2,0:T(8,128)(2,1)S(1)} %convert_element_type.99), channel_id=1, replica_groups=mesh['grp'=2,'dev'=16] {'grp'}, dimensions={0}, use_global_device_ids=true | all-gather | bytes 49152 | tf_op jit(solution)/shard_map/all_gather | solution.py:101
  102.8 28.0 %all-gather = bf16[64,128,16]{1,2,0:T(8,128)(2,1)S(1)} all-gather(bf16[4,128,16]{1,2,0:T(8,128)(2,1)S(1)} %fusion.23), channel_id=2, replica_groups=mesh['grp'=2,'dev'=16] {'dev'}, dimensions={0}, use_global_device_ids=true | all-gather | bytes 278528 | tf_op jit(solution)/shard_map/all_gather | solution.py:106
  132.9 2.9 %scatter_custom_fusion = f32[512,256]{1,0:T(8,128)S(1)} fusion(s32[512]{0:T(512)S(1)} %bitcast.223, f32[512,256]{1,0:T(8,128)} %copy.55, f32[]{:T(128)} %constant.33.clone.1), kind=kCustom, calls=%fused_computation.70 | custom fusion | bytes 524800 | tf_op jit(solution)/shard_map/scatter | solution.py:114
  135.8 2.4 fusion.24
  138.5 2.0 collective-permute-start.20
  140.6 2.9 %collective-permute-start.21 = (bf16[512,256]{1,0:T(8,128)(2,1)S(1)}, bf16[512,256]{1,0:T(8,128)(2,1)}, u32[]{:S(2)}, u32[]{:S(2)}) collective-permute-start(bf16[512,256]{1,0:T(8,128)(2,1)S(1)} %get-tuple-element.18), channel_id=1, source_target_pairs={{0,1},{1,2},{2,3},{3,4},{4,5},{5,6},{6,7},{7,8},{8,9},{9,10},{10,1... | collective-permute-start | bytes 786440 | tf_op jit(solution)/shard_map/ppermute | solution.py:17
  143.5 1.9 gather_fusion.2
  145.8 1.3 collective-permute-start.24
  147.1 1.3 collective-permute-start.25
  148.4 2.2 collective-permute-start.26
  151.7 1.8 collective-permute-start.27
  154.1 2.3 collective-permute-start.28
  157.1 3.0 %collective-permute-start.29 = (bf16[128,256]{0,1:T(8,128)(2,1)S(1)}, bf16[128,256]{0,1:T(8,128)(2,1)S(1)}, u32[]{:S(2)}, u32[]{:S(2)}) collective-permute-start(bf16[128,256]{0,1:T(8,128)(2,1)S(1)} %bitcast.215), channel_id=1, source_target_pairs={{0,3},{1,4},{2,5},{3,6},{4,7},{5,8},{6,9},{7,10},{8,11},{9,12},{10... | collective-permute-start | bytes 196616 | tf_op jit(solution)/shard_map/ppermute | solution.py:17
  174.1 2.0 collective-permute-done.33
  179.9 5.8 %collective-permute-done.35 = bf16[128,256]{0,1:T(8,128)(2,1)S(1)} collective-permute-done((bf16[128,256]{0,1:T(8,128)(2,1)S(1)}, bf16[128,256]{0,1:T(8,128)(2,1)S(1)}, u32[]{:S(2)}, u32[]{:S(2)}) %collective-permute-start.35) | collective-permute-done | bytes 65568 | tf_op jit(solution)/shard_map/ppermute | solution.py:17
  186.3 2.0 copy.56
  191.5 1.3 convolution_multiply_fusion.5
  194.1 11.7 %reduce-scatter.5.cloned.1.call-done = f32[4,128,16]{1,2,0:T(8,128)} async-done(((f32[4,128,256]{1,2,0:T(8,128)}), f32[4,128,16]{1,2,0:T(8,128)}) %reduce-scatter.5.cloned.1.call-update) | async-done | bytes 32784 | tf_op jit(solution)/shard_map/reduce_scatter | solution.py:98
  206.6 4.4 %all_gather.21 = bf16[8,128,16]{1,2,0:T(8,128)(2,1)S(1)} all-gather(bf16[4,128,16]{1,2,0:T(8,128)(2,1)S(1)} %convert_element_type.107), channel_id=1, replica_groups=mesh['grp'=2,'dev'=16] {'grp'}, dimensions={0}, use_global_device_ids=true | all-gather | bytes 49152 | tf_op jit(solution)/shard_map/all_gather | solution.py:101
  211.8 20.1 %all-gather.1 = bf16[64,128,16]{1,2,0:T(8,128)(2,1)S(1)} all-gather(bf16[4,128,16]{1,2,0:T(8,128)(2,1)S(1)} %fusion.22), channel_id=3, replica_groups=mesh['grp'=2,'dev'=16] {'dev'}, dimensions={0}, use_global_device_ids=true | all-gather | bytes 278528 | tf_op jit(solution)/shard_map/all_gather | solution.py:106
  233.2 2.4 scatter_custom_fusion.1
  235.6 2.7 %add_add_fusion = (f32[512,256]{1,0:T(8,128)}, f32[512,256]{1,0:T(8,128)}) fusion(f32[512,256]{1,0:T(8,128)} %get-tuple-element.19, f32[]{:T(128)S(6)} %div.39, f32[]{:T(128)S(6)} %mul.207, f32[]{:T(128)S(6)} %div.37, f32[]{:T(128)S(6)} %mul.171, f32[512,256]{1,0:T(8,128)S(1)} %copy-done.11, f32[]{:T(128)S(6)} %div.30, ...), kind=kOutput, calls=%fused_computation.61 | convolution fusion | flops 136314880 | bytes 4456476 | tf_op jit(solution)/shard_map/dot_general | solution.py:75
  (172 shorter events, 56.9 us)
Async XLA Ops:
  7.2 95.4 %copy-start = (bf16[4,4,128,128]{3,2,1,0:T(8,128)(2,1)S(1)}, bf16[4,4,128,128]{3,2,1,0:T(8,128)(2,1)}, u32[]{:S(2)}) copy-start(bf16[4,4,128,128]{3,2,1,0:T(8,128)(2,1)} %param.22) | copy-start | bytes 1572868
  7.2 89.6 %reduce-scatter.3.cloned.1.call-start = ((), (), s32[]{:S(2)}) async-start(), calls=%async_computation.2 | async-start | bytes 557056 | tf_op jit(solution)/shard_map/reduce_scatter | solution.py:98
  9.7 2.0 copy-start.1
  11.7 15.0 %copy-start.6 = (bf16[1,128,128]{2,1,0:T(8,128)(2,1)S(1)}, bf16[1,128,128]{2,1,0:T(8,128)(2,1)}, u32[]{:S(2)}) copy-start(bf16[1,128,128]{2,1,0:T(8,128)(2,1)} %param.18) | copy-start | bytes 98308
  12.0 26.9 %collective-permute-start.8 = (bf16[128,256]{0,1:T(8,128)(2,1)S(1)}, bf16[128,256]{0,1:T(8,128)(2,1)S(1)}, u32[]{:S(2)}, u32[]{:S(2)}) collective-permute-start(bf16[128,256]{0,1:T(8,128)(2,1)S(1)} %bitcast.198), channel_id=1, source_target_pairs={{0,8},{1,9},{2,10},{3,11},{4,12},{5,13},{6,14},{7,15},{16,24},{17,... | collective-permute-start | bytes 196616 | tf_op jit(solution)/shard_map/ppermute | solution.py:17
  18.0 24.4 %collective-permute-start.9 = (bf16[128,256]{0,1:T(8,128)(2,1)S(1)}, bf16[128,256]{0,1:T(8,128)(2,1)S(1)}, u32[]{:S(2)}, u32[]{:S(2)}) collective-permute-start(bf16[128,256]{0,1:T(8,128)(2,1)S(1)} %bitcast.199), channel_id=1, source_target_pairs={{0,7},{1,8},{2,9},{3,10},{4,11},{5,12},{6,13},{7,14},{8,15},{16,23... | collective-permute-start | bytes 196616 | tf_op jit(solution)/shard_map/ppermute | solution.py:17
  21.6 22.7 %collective-permute-start.10 = (bf16[128,256]{0,1:T(8,128)(2,1)S(1)}, bf16[128,256]{0,1:T(8,128)(2,1)S(1)}, u32[]{:S(2)}, u32[]{:S(2)}) collective-permute-start(bf16[128,256]{0,1:T(8,128)(2,1)S(1)} %bitcast.200), channel_id=1, source_target_pairs={{0,6},{1,7},{2,8},{3,9},{4,10},{5,11},{6,12},{7,13},{8,14},{9,15},... | collective-permute-start | bytes 196616 | tf_op jit(solution)/shard_map/ppermute | solution.py:17
  23.7 22.5 %collective-permute-start.11 = (bf16[128,256]{0,1:T(8,128)(2,1)S(1)}, bf16[128,256]{0,1:T(8,128)(2,1)S(1)}, u32[]{:S(2)}, u32[]{:S(2)}) collective-permute-start(bf16[128,256]{0,1:T(8,128)(2,1)S(1)} %bitcast.201), channel_id=1, source_target_pairs={{0,5},{1,6},{2,7},{3,8},{4,9},{5,10},{6,11},{7,12},{8,13},{9,14},{... | collective-permute-start | bytes 196616 | tf_op jit(solution)/shard_map/ppermute | solution.py:17
  25.0 23.1 %collective-permute-start.12 = (bf16[128,256]{0,1:T(8,128)(2,1)S(1)}, bf16[128,256]{0,1:T(8,128)(2,1)S(1)}, u32[]{:S(2)}, u32[]{:S(2)}) collective-permute-start(bf16[128,256]{0,1:T(8,128)(2,1)S(1)} %bitcast.202), channel_id=1, source_target_pairs={{0,4},{1,5},{2,6},{3,7},{4,8},{5,9},{6,10},{7,11},{8,12},{9,13},{1... | collective-permute-start | bytes 196616 | tf_op jit(solution)/shard_map/ppermute | solution.py:17
  28.4 177.4 %reduce-scatter.5.cloned.1.call-start = ((), (), s32[]{:S(2)}) async-start(), calls=%async_computation.3 | async-start | bytes 557056 | tf_op jit(solution)/shard_map/reduce_scatter | solution.py:98
  34.3 2.2 copy-start.14
  38.8 11.2 %collective-permute-start.13 = (bf16[128,256]{0,1:T(8,128)(2,1)S(1)}, bf16[128,256]{0,1:T(8,128)(2,1)S(1)}, u32[]{:S(2)}, u32[]{:S(2)}) collective-permute-start(bf16[128,256]{0,1:T(8,128)(2,1)S(1)} %bitcast.203), channel_id=1, source_target_pairs={{0,3},{1,4},{2,5},{3,6},{4,7},{5,8},{6,9},{7,10},{8,11},{9,12},{10... | collective-permute-start | bytes 196616 | tf_op jit(solution)/shard_map/ppermute | solution.py:17
  42.4 9.6 %collective-permute-start.14 = (bf16[128,256]{0,1:T(8,128)(2,1)S(1)}, bf16[128,256]{0,1:T(8,128)(2,1)S(1)}, u32[]{:S(2)}, u32[]{:S(2)}) collective-permute-start(bf16[128,256]{0,1:T(8,128)(2,1)S(1)} %bitcast.204), channel_id=1, source_target_pairs={{3,0},{4,1},{5,2},{6,3},{7,4},{8,5},{9,6},{10,7},{11,8},{12,9},{13... | collective-permute-start | bytes 196616 | tf_op jit(solution)/shard_map/ppermute | solution.py:17
  44.3 9.6 %collective-permute-start.15 = (bf16[128,256]{0,1:T(8,128)(2,1)S(1)}, bf16[128,256]{0,1:T(8,128)(2,1)S(1)}, u32[]{:S(2)}, u32[]{:S(2)}) collective-permute-start(bf16[128,256]{0,1:T(8,128)(2,1)S(1)} %bitcast.205), channel_id=1, source_target_pairs={{4,0},{5,1},{6,2},{7,3},{8,4},{9,5},{10,6},{11,7},{12,8},{13,9},{1... | collective-permute-start | bytes 196616 | tf_op jit(solution)/shard_map/ppermute | solution.py:17
  46.2 11.1 %collective-permute-start.16 = (bf16[128,256]{0,1:T(8,128)(2,1)S(1)}, bf16[128,256]{0,1:T(8,128)(2,1)S(1)}, u32[]{:S(2)}, u32[]{:S(2)}) collective-permute-start(bf16[128,256]{0,1:T(8,128)(2,1)S(1)} %bitcast.206), channel_id=1, source_target_pairs={{5,0},{6,1},{7,2},{8,3},{9,4},{10,5},{11,6},{12,7},{13,8},{14,9},{... | collective-permute-start | bytes 196616 | tf_op jit(solution)/shard_map/ppermute | solution.py:17
  48.1 15.2 %collective-permute-start.17 = (bf16[128,256]{0,1:T(8,128)(2,1)S(1)}, bf16[128,256]{0,1:T(8,128)(2,1)S(1)}, u32[]{:S(2)}, u32[]{:S(2)}) collective-permute-start(bf16[128,256]{0,1:T(8,128)(2,1)S(1)} %bitcast.207), channel_id=1, source_target_pairs={{6,0},{7,1},{8,2},{9,3},{10,4},{11,5},{12,6},{13,7},{14,8},{15,9},... | collective-permute-start | bytes 196616 | tf_op jit(solution)/shard_map/ppermute | solution.py:17
  50.1 16.8 %collective-permute-start.18 = (bf16[128,256]{0,1:T(8,128)(2,1)S(1)}, bf16[128,256]{0,1:T(8,128)(2,1)S(1)}, u32[]{:S(2)}, u32[]{:S(2)}) collective-permute-start(bf16[128,256]{0,1:T(8,128)(2,1)S(1)} %bitcast.208), channel_id=1, source_target_pairs={{7,0},{8,1},{9,2},{10,3},{11,4},{12,5},{13,6},{14,7},{15,8},{23,16... | collective-permute-start | bytes 196616 | tf_op jit(solution)/shard_map/ppermute | solution.py:17
  52.0 19.6 %collective-permute-start.19 = (bf16[128,256]{0,1:T(8,128)(2,1)S(1)}, bf16[128,256]{0,1:T(8,128)(2,1)S(1)}, u32[]{:S(2)}, u32[]{:S(2)}) collective-permute-start(bf16[128,256]{0,1:T(8,128)(2,1)S(1)} %bitcast.209), channel_id=1, source_target_pairs={{8,0},{9,1},{10,2},{11,3},{12,4},{13,5},{14,6},{15,7},{24,16},{25,... | collective-permute-start | bytes 196616 | tf_op jit(solution)/shard_map/ppermute | solution.py:17
  53.9 38.3 %collective-permute-start.1 = (bf16[512,256]{1,0:T(8,128)(2,1)S(1)}, bf16[512,256]{1,0:T(8,128)(2,1)}, u32[]{:S(2)}, u32[]{:S(2)}) collective-permute-start(bf16[512,256]{1,0:T(8,128)(2,1)S(1)} %fusion.53), channel_id=1, source_target_pairs={{0,2},{1,3},{2,4},{3,5},{4,6},{5,7},{6,8},{7,9},{8,10},{9,11},{10,... | collective-permute-start | bytes 786440 | tf_op jit(solution)/shard_map/ppermute | solution.py:17
  57.4 19.4 %collective-permute-start = (f32[512,64]{0,1:T(8,128)}, f32[512,64]{0,1:T(8,128)S(1)}, u32[]{:S(2)}, u32[]{:S(2)}) collective-permute-start(f32[512,64]{0,1:T(8,128)} %param.12), channel_id=1, source_target_pairs={{0,2},{1,3},{2,4},{3,5},{4,6},{5,7},{6,8},{7,9},{8,10},{9,11},{10,... | collective-permute-start | bytes 393224 | tf_op jit(solution)/shard_map/ppermute | solution.py:17
  63.4 31.3 %collective-permute-start.3 = (bf16[512,256]{1,0:T(8,128)(2,1)S(1)}, bf16[512,256]{1,0:T(8,128)(2,1)}, u32[]{:S(2)}, u32[]{:S(2)}) collective-permute-start(bf16[512,256]{1,0:T(8,128)(2,1)S(1)} %fusion.53), channel_id=1, source_target_pairs={{0,1},{1,2},{2,3},{3,4},{4,5},{5,6},{6,7},{7,8},{8,9},{9,10},{10,1... | collective-permute-start | bytes 786440 | tf_op jit(solution)/shard_map/ppermute | solution.py:17
  66.8 13.4 %collective-permute-start.2 = (f32[512,64]{0,1:T(8,128)}, f32[512,64]{0,1:T(8,128)}, u32[]{:S(2)}, u32[]{:S(2)}) collective-permute-start(f32[512,64]{0,1:T(8,128)} %param.12), channel_id=1, source_target_pairs={{0,1},{1,2},{2,3},{3,4},{4,5},{5,6},{6,7},{7,8},{8,9},{9,10},{10,1... | collective-permute-start | bytes 393224 | tf_op jit(solution)/shard_map/ppermute | solution.py:17
  71.6 21.9 %collective-permute-start.7 = (bf16[512,256]{1,0:T(8,128)(2,1)S(1)}, bf16[512,256]{1,0:T(8,128)(2,1)}, u32[]{:S(2)}, u32[]{:S(2)}) collective-permute-start(bf16[512,256]{1,0:T(8,128)(2,1)S(1)} %fusion.53), channel_id=1, source_target_pairs={{2,0},{3,1},{4,2},{5,3},{6,4},{7,5},{8,6},{9,7},{10,8},{11,9},{12,... | collective-permute-start | bytes 786440 | tf_op jit(solution)/shard_map/ppermute | solution.py:17
  76.7 9.1 %collective-permute-start.6 = (f32[512,64]{0,1:T(8,128)}, f32[512,64]{0,1:T(8,128)S(1)}, u32[]{:S(2)}, u32[]{:S(2)}) collective-permute-start(f32[512,64]{0,1:T(8,128)} %param.12), channel_id=1, source_target_pairs={{2,0},{3,1},{4,2},{5,3},{6,4},{7,5},{8,6},{9,7},{10,8},{11,9},{12,... | collective-permute-start | bytes 393224 | tf_op jit(solution)/shard_map/ppermute | solution.py:17
  80.2 12.0 %copy-start.4 = (bf16[512,512]{1,0:T(8,128)(2,1)}, bf16[512,512]{1,0:T(8,128)(2,1)S(1)}, u32[]{:S(2)}) copy-start(bf16[512,512]{1,0:T(8,128)(2,1)S(1)} %exponential_convert_fusion.3) | copy-start | bytes 1572868
  80.2 55.6 %collective-permute-start.5 = (bf16[512,256]{1,0:T(8,128)(2,1)S(1)}, bf16[512,256]{1,0:T(8,128)(2,1)}, u32[]{:S(2)}, u32[]{:S(2)}) collective-permute-start(bf16[512,256]{1,0:T(8,128)(2,1)S(1)} %fusion.53), channel_id=1, source_target_pairs={{1,0},{2,1},{3,2},{4,3},{5,4},{6,5},{7,6},{8,7},{9,8},{10,9},{11,1... | collective-permute-start | bytes 786440 | tf_op jit(solution)/shard_map/ppermute | solution.py:17
  84.6 10.2 %copy-start.2 = (bf16[512,512]{1,0:T(8,128)(2,1)}, bf16[512,512]{1,0:T(8,128)(2,1)S(1)}, u32[]{:S(2)}) copy-start(bf16[512,512]{1,0:T(8,128)(2,1)S(1)} %exponential_convert_fusion.2) | copy-start | bytes 1572868
  85.8 3.4 %collective-permute-start.4 = (f32[512,64]{0,1:T(8,128)}, f32[512,64]{0,1:T(8,128)S(1)}, u32[]{:S(2)}, u32[]{:S(2)}) collective-permute-start(f32[512,64]{0,1:T(8,128)} %param.12), channel_id=1, source_target_pairs={{1,0},{2,1},{3,2},{4,3},{5,4},{6,5},{7,6},{8,7},{9,8},{10,9},{11,1... | collective-permute-start | bytes 393224 | tf_op jit(solution)/shard_map/ppermute | solution.py:17
  132.9 2.9 %copy-start.10 = (f32[512,256]{1,0:T(8,128)S(1)}, f32[512,256]{1,0:T(8,128)}, u32[]{:S(2)}) copy-start(f32[512,256]{1,0:T(8,128)} %param.13) | copy-start | bytes 1572868
  138.5 50.9 %collective-permute-start.20 = (bf16[512,256]{1,0:T(8,128)(2,1)S(1)}, bf16[512,256]{1,0:T(8,128)(2,1)}, u32[]{:S(2)}, u32[]{:S(2)}) collective-permute-start(bf16[512,256]{1,0:T(8,128)(2,1)S(1)} %get-tuple-element.18), channel_id=1, source_target_pairs={{0,2},{1,3},{2,4},{3,5},{4,6},{5,7},{6,8},{7,9},{8,10},{9,11},{10,... | collective-permute-start | bytes 786440 | tf_op jit(solution)/shard_map/ppermute | solution.py:17
  140.6 52.3 %collective-permute-start.21 = (bf16[512,256]{1,0:T(8,128)(2,1)S(1)}, bf16[512,256]{1,0:T(8,128)(2,1)}, u32[]{:S(2)}, u32[]{:S(2)}) collective-permute-start(bf16[512,256]{1,0:T(8,128)(2,1)S(1)} %get-tuple-element.18), channel_id=1, source_target_pairs={{0,1},{1,2},{2,3},{3,4},{4,5},{5,6},{6,7},{7,8},{8,9},{9,10},{10,1... | collective-permute-start | bytes 786440 | tf_op jit(solution)/shard_map/ppermute | solution.py:17
  145.5 5.2 %copy-start.8 = (bf16[1,128,128]{2,1,0:T(8,128)(2,1)S(1)}, bf16[1,128,128]{2,1,0:T(8,128)(2,1)}, u32[]{:S(2)}) copy-start(bf16[1,128,128]{2,1,0:T(8,128)(2,1)} %param.18) | copy-start | bytes 98308
  145.7 5.0 %copy-start.19 = (f32[4]{0:T(128)S(1)}, f32[4]{0:T(128)}, u32[]{:S(2)}) copy-start(f32[4]{0:T(128)} %copy-done.18) | copy-start | bytes 52
  145.8 5.9 %collective-permute-start.24 = (bf16[128,256]{0,1:T(8,128)(2,1)S(1)}, bf16[128,256]{0,1:T(8,128)(2,1)S(1)}, u32[]{:S(2)}, u32[]{:S(2)}) collective-permute-start(bf16[128,256]{0,1:T(8,128)(2,1)S(1)} %bitcast.210), channel_id=1, source_target_pairs={{0,8},{1,9},{2,10},{3,11},{4,12},{5,13},{6,14},{7,15},{16,24},{17,... | collective-permute-start | bytes 196616 | tf_op jit(solution)/shard_map/ppermute | solution.py:17
  147.1 7.1 %collective-permute-start.25 = (bf16[128,256]{0,1:T(8,128)(2,1)S(1)}, bf16[128,256]{0,1:T(8,128)(2,1)S(1)}, u32[]{:S(2)}, u32[]{:S(2)}) collective-permute-start(bf16[128,256]{0,1:T(8,128)(2,1)S(1)} %bitcast.211), channel_id=1, source_target_pairs={{0,7},{1,8},{2,9},{3,10},{4,11},{5,12},{6,13},{7,14},{8,15},{16,23... | collective-permute-start | bytes 196616 | tf_op jit(solution)/shard_map/ppermute | solution.py:17
  148.4 8.8 %collective-permute-start.26 = (bf16[128,256]{0,1:T(8,128)(2,1)S(1)}, bf16[128,256]{0,1:T(8,128)(2,1)S(1)}, u32[]{:S(2)}, u32[]{:S(2)}) collective-permute-start(bf16[128,256]{0,1:T(8,128)(2,1)S(1)} %bitcast.212), channel_id=1, source_target_pairs={{0,6},{1,7},{2,8},{3,9},{4,10},{5,11},{6,12},{7,13},{8,14},{9,15},... | collective-permute-start | bytes 196616 | tf_op jit(solution)/shard_map/ppermute | solution.py:17
  151.7 9.0 %collective-permute-start.27 = (bf16[128,256]{0,1:T(8,128)(2,1)S(1)}, bf16[128,256]{0,1:T(8,128)(2,1)S(1)}, u32[]{:S(2)}, u32[]{:S(2)}) collective-permute-start(bf16[128,256]{0,1:T(8,128)(2,1)S(1)} %bitcast.213), channel_id=1, source_target_pairs={{0,5},{1,6},{2,7},{3,8},{4,9},{5,10},{6,11},{7,12},{8,13},{9,14},{... | collective-permute-start | bytes 196616 | tf_op jit(solution)/shard_map/ppermute | solution.py:17
  154.1 8.5 %collective-permute-start.28 = (bf16[128,256]{0,1:T(8,128)(2,1)S(1)}, bf16[128,256]{0,1:T(8,128)(2,1)S(1)}, u32[]{:S(2)}, u32[]{:S(2)}) collective-permute-start(bf16[128,256]{0,1:T(8,128)(2,1)S(1)} %bitcast.214), channel_id=1, source_target_pairs={{0,4},{1,5},{2,6},{3,7},{4,8},{5,9},{6,10},{7,11},{8,12},{9,13},{1... | collective-permute-start | bytes 196616 | tf_op jit(solution)/shard_map/ppermute | solution.py:17
  157.1 7.5 %collective-permute-start.29 = (bf16[128,256]{0,1:T(8,128)(2,1)S(1)}, bf16[128,256]{0,1:T(8,128)(2,1)S(1)}, u32[]{:S(2)}, u32[]{:S(2)}) collective-permute-start(bf16[128,256]{0,1:T(8,128)(2,1)S(1)} %bitcast.215), channel_id=1, source_target_pairs={{0,3},{1,4},{2,5},{3,6},{4,7},{5,8},{6,9},{7,10},{8,11},{9,12},{10... | collective-permute-start | bytes 196616 | tf_op jit(solution)/shard_map/ppermute | solution.py:17
  160.8 5.8 %collective-permute-start.30 = (bf16[128,256]{0,1:T(8,128)(2,1)S(1)}, bf16[128,256]{0,1:T(8,128)(2,1)S(1)}, u32[]{:S(2)}, u32[]{:S(2)}) collective-permute-start(bf16[128,256]{0,1:T(8,128)(2,1)S(1)} %bitcast.216), channel_id=1, source_target_pairs={{3,0},{4,1},{5,2},{6,3},{7,4},{8,5},{9,6},{10,7},{11,8},{12,9},{13... | collective-permute-start | bytes 196616 | tf_op jit(solution)/shard_map/ppermute | solution.py:17
  162.7 6.8 %collective-permute-start.31 = (bf16[128,256]{0,1:T(8,128)(2,1)S(1)}, bf16[128,256]{0,1:T(8,128)(2,1)S(1)}, u32[]{:S(2)}, u32[]{:S(2)}) collective-permute-start(bf16[128,256]{0,1:T(8,128)(2,1)S(1)} %bitcast.217), channel_id=1, source_target_pairs={{4,0},{5,1},{6,2},{7,3},{8,4},{9,5},{10,6},{11,7},{12,8},{13,9},{1... | collective-permute-start | bytes 196616 | tf_op jit(solution)/shard_map/ppermute | solution.py:17
  164.6 7.6 %collective-permute-start.32 = (bf16[128,256]{0,1:T(8,128)(2,1)S(1)}, bf16[128,256]{0,1:T(8,128)(2,1)S(1)}, u32[]{:S(2)}, u32[]{:S(2)}) collective-permute-start(bf16[128,256]{0,1:T(8,128)(2,1)S(1)} %bitcast.218), channel_id=1, source_target_pairs={{5,0},{6,1},{7,2},{8,3},{9,4},{10,5},{11,6},{12,7},{13,8},{14,9},{... | collective-permute-start | bytes 196616 | tf_op jit(solution)/shard_map/ppermute | solution.py:17
  166.5 9.5 %collective-permute-start.33 = (bf16[128,256]{0,1:T(8,128)(2,1)S(1)}, bf16[128,256]{0,1:T(8,128)(2,1)S(1)}, u32[]{:S(2)}, u32[]{:S(2)}) collective-permute-start(bf16[128,256]{0,1:T(8,128)(2,1)S(1)} %bitcast.219), channel_id=1, source_target_pairs={{6,0},{7,1},{8,2},{9,3},{10,4},{11,5},{12,6},{13,7},{14,8},{15,9},... | collective-permute-start | bytes 196616 | tf_op jit(solution)/shard_map/ppermute | solution.py:17
  169.5 8.5 %collective-permute-start.34 = (bf16[128,256]{0,1:T(8,128)(2,1)S(1)}, bf16[128,256]{0,1:T(8,128)(2,1)S(1)}, u32[]{:S(2)}, u32[]{:S(2)}) collective-permute-start(bf16[128,256]{0,1:T(8,128)(2,1)S(1)} %bitcast.220), channel_id=1, source_target_pairs={{7,0},{8,1},{9,2},{10,3},{11,4},{12,5},{13,6},{14,7},{15,8},{23,16... | collective-permute-start | bytes 196616 | tf_op jit(solution)/shard_map/ppermute | solution.py:17
  172.2 13.5 %collective-permute-start.35 = (bf16[128,256]{0,1:T(8,128)(2,1)S(1)}, bf16[128,256]{0,1:T(8,128)(2,1)S(1)}, u32[]{:S(2)}, u32[]{:S(2)}) collective-permute-start(bf16[128,256]{0,1:T(8,128)(2,1)S(1)} %bitcast.221), channel_id=1, source_target_pairs={{8,0},{9,1},{10,2},{11,3},{12,4},{13,5},{14,6},{15,7},{24,16},{25,... | collective-permute-start | bytes 196616 | tf_op jit(solution)/shard_map/ppermute | solution.py:17
  176.1 15.4 %collective-permute-start.23 = (bf16[512,256]{1,0:T(8,128)(2,1)S(1)}, bf16[512,256]{1,0:T(8,128)(2,1)}, u32[]{:S(2)}, u32[]{:S(2)}) collective-permute-start(bf16[512,256]{1,0:T(8,128)(2,1)S(1)} %get-tuple-element.18), channel_id=1, source_target_pairs={{2,0},{3,1},{4,2},{5,3},{6,4},{7,5},{8,6},{9,7},{10,8},{11,9},{12,... | collective-permute-start | bytes 786440 | tf_op jit(solution)/shard_map/ppermute | solution.py:17
  178.0 57.6 %collective-permute-start.22 = (bf16[512,256]{1,0:T(8,128)(2,1)S(1)}, bf16[512,256]{1,0:T(8,128)(2,1)}, u32[]{:S(2)}, u32[]{:S(2)}) collective-permute-start(bf16[512,256]{1,0:T(8,128)(2,1)S(1)} %get-tuple-element.18), channel_id=1, source_target_pairs={{1,0},{2,1},{3,2},{4,3},{5,4},{6,5},{7,6},{8,7},{9,8},{10,9},{11,1... | collective-permute-start | bytes 786440 | tf_op jit(solution)/shard_map/ppermute | solution.py:17
  233.2 2.4 copy-start.11
  (12 other events, 10.7 us)
Sparse Core Ops, SparseCore 0:
  28.5 57.2 reduce-scatter.2
  151.8 53.9 reduce-scatter.4
